TPU v7x, 32 devices: a whole 2x2x4 slice. The times are simulated.
32 devices in a mesh: shots: 2 (over y), wide: 16 (over z, x, core).
Axes of the slice: x: 2, y: 2, z: 4, core: 2. Of those that a mesh axis runs over, the one named last changes fastest.
Arguments:
- src_now: float32 [32, 64, 128], P('wide', 'shots'), parts along dimension 1, may hold values from -6 to 6
- src_old: float32 [32, 64, 128], P('wide', 'shots'), parts along dimension 1, may hold values from -6 to 6
- rcv_now: float32 [32, 256, 32], P('wide', 'shots'), parts along dimension 1, may hold values from -6 to 6
- rcv_old: float32 [32, 256, 32], P('wide', 'shots'), parts along dimension 1, may hold values from -6 to 6
- medium: float32 [3, 32, 128, 32], P(None, 'wide'), may hold values from 0.04 to 0.24
- wavelet: float32 [4], replicated, may hold values from -4 to 4
- shot: int32 [6], P('shots'), parts along dimension 0, may hold values from 0 to 31
- traces: float32 [32, 128, 4], P('wide', 'shots'), parts along dimension 1, may hold values from -6 to 6
- rec_x: int32 [32, 128], P('wide', 'shots'), parts along dimension 1, may hold values from 0 to 31
- lag_order: int32 [33], replicated, may hold values from 0 to 32, each once
Outputs:
- src_next: float32 [32, 64, 128], P('wide', 'shots'), parts along dimension 1
- src_prior: float32 [32, 64, 128], P('wide', 'shots'), parts along dimension 1
- rcv_next: float32 [32, 256, 32], P('wide', 'shots'), parts along dimension 1
- rcv_prior: float32 [32, 256, 32], P('wide', 'shots'), parts along dimension 1
- image: float32 [66, 32, 128, 32], P('shots', 'wide'), parts along dimension 0
There are 2 independent parts, one for each index of `shots`. A program takes and returns all parts, laid end to end along the dimension named above; an argument that names none is the same for every part. Nothing has to cross between parts.
Inputs may be any that keep to these rules, and one draw needn't show every extreme that they name: `lag_order`: each of the 33 lag slots once.
All inputs are finite; a program needn't handle non-finite values.
Results may differ from a plain program's by a relative error of at most 0.0003.
Values sent between devices are 32-bit elements; how exact they have to be, the bound alone decides.
A program may use at most 64 MiB of HBM per device.

v0:
```python
import functools
import math

import jax
import jax.numpy as jnp
from jax import lax
from jax.experimental import pallas as pl
from jax.experimental.pallas import tpu as pltpu
from jax.sharding import PartitionSpec as P

REACH = 2
EDGE = 8
OUTER, INNER, CENTRE = -1.0 / 12.0, 4.0 / 3.0, -2.5
SRC, RCV = 0, 1


def second(window):
    return (
        OUTER * (window(-2) + window(2)) + INNER * (window(-1) + window(1)) + CENTRE * window(0)
    )


def window_kernel(
    devices,
    src_now_in,
    src_old_in,
    rcv_now_in,
    rcv_old_in,
    medium_in,
    wavelet_in,
    shot_in,
    traces_in,
    rec_x_in,
    lag_order_in,
    src_next,
    src_prior,
    rcv_next,
    rcv_prior,
    board,
    src_now,
    src_old,
    rcv_old,
    medium,
    wavelet,
    shot,
    traces,
    rec_x,
    lag_order,
    padded,
    staged,
    landed,
    levels,
    partial,
    surface,
    spot,
    leaving,
    returned,
    out_send,
    out_recv,
    back_send,
    back_recv,
    halo_send,
    halo_recv,
    load_sems,
):
    me = lax.axis_index("wide")
    slab_x, cells_y, cells_z = src_now.shape
    slab_y, cells_x, _ = rcv_old.shape
    steps = wavelet.shape[0]
    span = slab_y + 2 * REACH
    rows = staged.shape[0] // (devices * slab_x)
    block = slab_x * rows
    back_rows = 2 * slab_x * slab_y
    inside = pl.ds(EDGE, cells_x)

    lags = lag_order.shape[0]
    half = (lags - 1) // 2
    middle = devices // 2
    far_first = sorted(range(1, devices), key=lambda distance: abs(distance - middle))

    loads = []
    for index, (source, target) in enumerate(
        (
            (src_now_in, src_now),
            (src_old_in, src_old),
            (rcv_now_in, levels.at[0, RCV, pl.ds(REACH, slab_y), inside]),
            (shot_in, shot),
            (traces_in, traces),
            (rec_x_in, rec_x),
            (rcv_old_in, rcv_old),
            (medium_in, medium),
            (wavelet_in, wavelet),
            (lag_order_in, lag_order),
        )
    ):
        loads.append(pltpu.make_async_copy(source, target, load_sems.at[index]))
    for load in loads[:3]:
        load.start()

    barrier = pltpu.get_barrier_semaphore()
    for distance in far_first:
        pl.semaphore_signal(
            barrier,
            inc=1,
            device_id={"wide": lax.rem(me + distance, devices)},
            device_id_type=MESH,
        )
    for load in loads[3:]:
        load.start()

    zero_edge = jnp.zeros((EDGE, cells_z), jnp.float32)
    zero_plane = jnp.zeros((cells_x, cells_z), jnp.float32)
    zero_half = jnp.zeros((half, cells_z), jnp.float32)
    for snap in range(padded.shape[0]):
        for field in (SRC, RCV):
            for y in range(slab_y):
                padded[snap, field, y, 0:half, :] = zero_half
                padded[snap, field, y, half + cells_x : 2 * half + cells_x, :] = zero_half
    for level in range(steps):
        for field in (SRC, RCV):
            for y in range(REACH, REACH + slab_y):
                levels[level, field, y, 0:EDGE, :] = zero_edge
                levels[level, field, y, EDGE + cells_x : EDGE + cells_x + EDGE, :] = zero_edge

    @pl.when(me == 0)
    def _():
        for level in range(steps):
            for field in (SRC, RCV):
                for y in range(REACH):
                    levels[level, field, y, inside, :] = zero_plane

    @pl.when(me == devices - 1)
    def _():
        for level in range(steps):
            for field in (SRC, RCV):
                for y in range(REACH):
                    levels[level, field, REACH + slab_y + y, inside, :] = zero_plane

    loads[0].wait()
    loads[1].wait()

    for peer in range(devices):
        first = peer * slab_y - REACH
        low, high = max(first, 0), min(first + span, cells_y)
        for x in range(slab_x):
            base = (peer * slab_x + x) * rows
            if low > first or high < first + span:
                staged[base : base + rows, :] = jnp.zeros((rows, cells_z), jnp.float32)
            staged[base + low - first : base + high - first, :] = src_now[x, low:high, :]
            staged[base + span : base + span + slab_y, :] = src_old[
                x, peer * slab_y : (peer + 1) * slab_y, :
            ]

    for load in loads[3:]:
        load.wait()
    row_at = lax.broadcasted_iota(jnp.int32, (cells_x, cells_z), 0)
    lane_at = lax.broadcasted_iota(jnp.int32, (cells_x, cells_z), 1)
    column = ((row_at == shot[0]) & (lane_at == shot[2])).astype(jnp.float32)
    for y in range(slab_y):
        spot[y] = column * (me * slab_y + y == shot[1]).astype(jnp.float32)
    x_at = lax.broadcasted_iota(jnp.int32, (cells_x, traces.shape[2]), 0)
    for y in range(slab_y):
        onehot = (x_at == rec_x[y : y + 1, :]).astype(jnp.float32)
        for step in range(steps):
            total = jnp.sum(onehot * traces[y, step : step + 1, :], axis=1, keepdims=True)
            surface[step, y] = jnp.where(lane_at == 0, total, 0.0)
    loads[2].wait()

    pl.semaphore_wait(barrier, devices - 1)

    def out_copy(peer):
        return pltpu.make_async_remote_copy(
            src_ref=staged.at[pl.ds(pl.multiple_of(peer * block, 8), block)],
            dst_ref=landed.at[pl.ds(pl.multiple_of(me * block, 8), block)],
            send_sem=out_send,
            recv_sem=out_recv,
            device_id={"wide": peer},
            device_id_type=MESH,
        )

    def halo_copy(field, level, side):
        first = slab_y if side == 0 else REACH
        source = levels.at[level, field, pl.ds(first, REACH), inside]
        into = 0 if side == 0 else REACH + slab_y
        peer = me + 1 if side == 0 else me - 1
        return pltpu.make_async_remote_copy(
            src_ref=source,
            dst_ref=levels.at[level, field, pl.ds(into, REACH), inside],
            send_sem=halo_send.at[field, level, side],
            recv_sem=halo_recv.at[field, level, side],
            device_id={"wide": peer},
            device_id_type=MESH,
        )

    def each_side(field, level, act):
        @pl.when(me < devices - 1)
        def _():
            act(0)

        @pl.when(me > 0)
        def _():
            act(1)

    def send_halo(field, level):
        each_side(field, level, lambda side: halo_copy(field, level, side).start())

    def wait_halo(field, level):
        each_side(field, level, lambda side: halo_copy(field, level, 1 - side).wait_recv())

    def wait_sent(field, level):
        each_side(field, level, lambda side: halo_copy(field, level, side).wait_send())

    for distance in far_first:
        out_copy(lax.rem(me + distance, devices)).start()

    send_halo(RCV, 0)

    own = pl.ds(pl.multiple_of(me * block, 8), block)
    landed[own, :] = staged[own, :]

    def older(field, level, y):
        if level > 0:
            return levels[level - 1, field, REACH + y, inside, :]
        if field == RCV:
            return rcv_old[y]
        return landed[pl.ds(span + y, cells_x, stride=rows), :]

    def local(field, level):
        for y in range(slab_y):
            centre = levels[level, field, REACH + y, inside, :]

            def along_x(shift):
                if shift == 0:
                    return centre
                return levels[level, field, REACH + y, pl.ds(EDGE + shift, cells_x), :]

            def along_z(shift):
                if shift == 0:
                    return centre
                turned = pltpu.roll(centre, (-shift) % cells_z, 1)
                kept = lane_at >= -shift if shift < 0 else lane_at < cells_z - shift
                return jnp.where(kept, turned, 0.0)

            partial[field, y] = (
                2.0 * centre
                - older(field, level, y)
                + medium[0, y] * second(along_x)
                + medium[2, y] * second(along_z)
            )

    def finish(field, level):
        for y in range(slab_y):
            def along_y(shift):
                return levels[level, field, REACH + y + shift, inside, :]

            if field == SRC:
                added = -wavelet[level] * spot[y]
            else:
                added = surface[level, y]
            levels[level + 1, field, REACH + y, inside, :] = (
                partial[field, y] + medium[1, y] * second(along_y) + added
            )

    local(RCV, 0)
    wait_halo(RCV, 0)
    finish(RCV, 0)
    send_halo(RCV, 1)
    local(RCV, 1)

    arrived = landed.at[pl.ds(0, (devices - 1) * block)]
    pltpu.make_async_copy(arrived, arrived, out_recv).wait()
    for y in range(span):
        levels[0, SRC, y, inside, :] = landed[pl.ds(y, cells_x, stride=rows), :]
    local(SRC, 0)
    finish(SRC, 0)
    for level in range(1, steps):
        send_halo(SRC, level)
        local(SRC, level)
        wait_halo(RCV, level)
        finish(RCV, level)
        if level + 1 < steps:
            send_halo(RCV, level + 1)
            local(RCV, level + 1)
        wait_halo(SRC, level)
        finish(SRC, level)

    for back, level in enumerate((steps, steps - 1)):
        for x in range(slab_x):
            for y in range(slab_y):
                at = (back * slab_x + x) * slab_y + y
                leaving[pl.ds(at, devices, stride=back_rows), :] = levels[
                    level, SRC, REACH + y, pl.ds(EDGE + x, devices, stride=slab_x), :
                ]

    def back_copy(peer):
        return pltpu.make_async_remote_copy(
            src_ref=leaving.at[pl.ds(pl.multiple_of(peer * back_rows, 8), back_rows)],
            dst_ref=returned.at[pl.ds(pl.multiple_of(me * back_rows, 8), back_rows)],
            send_sem=back_send,
            recv_sem=back_recv,
            device_id={"wide": peer},
            device_id_type=MESH,
        )

    for distance in far_first:
        back_copy(lax.rem(me + distance, devices)).start()

    own_back = pl.ds(pl.multiple_of(me * back_rows, 8), back_rows)
    returned[own_back, :] = leaving[own_back, :]
    for y in range(slab_y):
        rcv_next[y] = levels[steps, RCV, REACH + y, inside, :]
        rcv_prior[y] = levels[steps - 1, RCV, REACH + y, inside, :]
        for field in (SRC, RCV):
            for snap in range(padded.shape[0]):
                padded[snap, field, y, half : half + cells_x, :] = levels[
                    2 * snap + 2, field, REACH + y, inside, :
                ]
    for plane in range(lags):
        slot = lag_order[plane]
        at_src = pl.ds(2 * half - slot, cells_x)
        at_rcv = pl.ds(slot, cells_x)
        for y in range(slab_y):
            total = None
            for snap in range(padded.shape[0]):
                product = padded[snap, SRC, y, at_src, :] * padded[snap, RCV, y, at_rcv, :]
                total = product if total is None else total + product
            board[plane, y] = total

    sent = staged.at[pl.ds(0, (devices - 1) * block)]
    pltpu.make_async_copy(sent, sent, out_send).wait()
    for level in range(steps):
        wait_sent(RCV, level)
        if level > 0:
            wait_sent(SRC, level)

    came = returned.at[pl.ds(0, (devices - 1) * back_rows)]
    pltpu.make_async_copy(came, came, back_recv).wait()
    for back, result in enumerate((src_next, src_prior)):
        for x in range(slab_x):
            for y in range(slab_y):
                at = (back * slab_x + x) * slab_y + y
                result[x, pl.ds(y, devices, stride=slab_y), :] = returned[
                    pl.ds(at, devices, stride=back_rows), :
                ]
    gone = leaving.at[pl.ds(0, (devices - 1) * back_rows)]
    pltpu.make_async_copy(gone, gone, back_send).wait()


def deliver_kernel(*refs):
    count = (len(refs) - 1) // 2
    copies = [
        pltpu.make_async_copy(refs[i], refs[count + i], refs[-1].at[i]) for i in range(count)
    ]
    for copy in copies:
        copy.start()
    for copy in copies:
        copy.wait()


MESH = pl.DeviceIdType.MESH


def solution(mesh):
    devices = mesh.shape["wide"]

    def on_device(
        src_now, src_old, rcv_now, rcv_old, medium, wavelet, shot, traces, rec_x, lag_order
    ):
        slab_x, cells_y, cells_z = src_now.shape
        slab_y, _, cells_x = rcv_now.shape
        steps = wavelet.shape[0]
        lags = lag_order.shape[0]
        half = (lags - 1) // 2
        span = slab_y + 2 * REACH
        rows = -(-(span + slab_y) // 8) * 8
        f32 = jnp.float32
        vmem = pl.BlockSpec(memory_space=pltpu.VMEM)
        hbm = pl.BlockSpec(memory_space=pltpu.HBM)
        src_shape = jax.ShapeDtypeStruct((slab_x, cells_y, cells_z), f32)
        rcv_shape = jax.ShapeDtypeStruct((slab_y, cells_x, cells_z), f32)
        board_shape = jax.ShapeDtypeStruct((lags, slab_y, cells_x, cells_z), f32)
        shapes = (src_shape, src_shape, rcv_shape, rcv_shape, board_shape)
        taken = steps // 2
        turn = lambda array: jnp.swapaxes(array, -1, -2)
        like = lambda array: pltpu.VMEM(array.shape, array.dtype)
        scalars = lambda array: pltpu.SMEM(array.shape, array.dtype)
        rcv_now, rcv_old, medium, traces = map(turn, (rcv_now, rcv_old, medium, traces))
        scratch = [
            like(src_now),
            like(src_old),
            like(rcv_old),
            like(medium),
            scalars(wavelet),
            scalars(shot),
            like(traces),
            like(rec_x),
            scalars(lag_order),
            pltpu.VMEM((taken, 2, slab_y, cells_x + 2 * half, cells_z), f32),
            pltpu.VMEM((cells_x * rows, cells_z), f32),
            pltpu.VMEM((cells_x * rows, cells_z), f32),
            pltpu.VMEM((steps + 1, 2, span, cells_x + 2 * EDGE, cells_z), f32),
            pltpu.VMEM((2, slab_y, cells_x, cells_z), f32),
            pltpu.VMEM((steps, slab_y, cells_x, cells_z), f32),
            pltpu.VMEM((slab_y, cells_x, cells_z), f32),
            pltpu.VMEM((devices * 2 * slab_x * slab_y, cells_z), f32),
            pltpu.VMEM((devices * 2 * slab_x * slab_y, cells_z), f32),
        ]
        held = sum(4 * math.prod(each.shape) for each in scratch + list(shapes))
        results = pl.pallas_call(
            functools.partial(window_kernel, devices),
            out_shape=shapes,
            in_specs=[hbm] * 10,
            out_specs=(vmem,) * 5,
            scratch_shapes=scratch
            + [pltpu.SemaphoreType.DMA] * 4
            + [
                pltpu.SemaphoreType.DMA((2, steps, 2)),
                pltpu.SemaphoreType.DMA((2, steps, 2)),
                pltpu.SemaphoreType.DMA((10,)),
            ],
            compiler_params=pltpu.CompilerParams(
                collective_id=0, has_side_effects=True, vmem_limit_bytes=held + (4 << 20)
            ),
            name="window",
        )(
            *(
                pltpu.with_memory_space_constraint(array, pltpu.HBM)
                for array in (
                    src_now,
                    src_old,
                    rcv_now,
                    rcv_old,
                    medium,
                    wavelet,
                    shot,
                    traces,
                    rec_x,
                    lag_order,
                )
            )
        )
        outs = pl.pallas_call(
            deliver_kernel,
            out_shape=shapes,
            in_specs=[vmem] * 5,
            out_specs=(hbm,) * 5,
            scratch_shapes=[pltpu.SemaphoreType.DMA((5,))],
            compiler_params=pltpu.CompilerParams(vmem_limit_bytes=held + (4 << 20)),
            name="deliver",
        )(*results)
        return outs[0], outs[1], turn(outs[2]), turn(outs[3]), turn(outs[4])

    return jax.shard_map(
        on_device,
        mesh=mesh,
        in_specs=(
            P("wide", "shots", None),
            P("wide", "shots", None),
            P("wide", "shots", None),
            P("wide", "shots", None),
            P(None, "wide", None, None),
            P(),
            P("shots"),
            P("wide", "shots", None),
            P("wide", "shots"),
            P(),
        ),
        out_specs=(
            P("wide", "shots", None),
            P("wide", "shots", None),
            P("wide", "shots", None),
            P("wide", "shots", None),
            P("shots", "wide", None, None),
        ),
        check_vma=False,
    )
```

profile of v0, /device:TPU:0, one launch (start us, length us, event | category | flops | bytes accessed | tf_op | source)
XLA Modules:
  0.0 25.3 jit_solution(11156499057668812402)
XLA Ops:
  0.6 23.6 %window.1 = (f32[2,32,128]{2,1,0:T(8,128)S(1)}, f32[2,32,128]{2,1,0:T(8,128)S(1)}, f32[2,32,128]{2,1,0:T(8,128)S(1)}, f32[2,32,128]{2,1,0:T(8,128)S(1)}, f32[33,2,32,128]{3,2,1,0:T(8,128)S(1)}) custom-call(f32[2,32,128]{2,1,0:T(8,128)} %src_now_in.1, f32[2,32,128]{2,1,0:T(8,128)} %src_old_in.1, f32[2,32,128]{2,1,0:T(8,128)} %bitcast.8, ...), custom_call_target="tpu_custom_call" | custom-call | tf_op jit(solution)/shard_map/window/pallas_call | solution.py:409
  24.3 1.1 %deliver.1 = (f32[2,32,128]{2,1,0:T(8,128)}, f32[2,32,128]{2,1,0:T(8,128)}, f32[2,32,128]{2,1,0:T(8,128)}, f32[2,32,128]{2,1,0:T(8,128)}, f32[33,2,32,128]{3,2,1,0:T(8,128)}) custom-call(f32[2,32,128]{2,1,0:T(8,128)S(1)} %get-tuple-element.15.refs_0_, f32[2,32,128]{2,1,0:T(8,128)S(1)} %get-tuple-element.16.refs_1_, ...), custom_call_target="tpu_custom_call" | custom-call | tf_op jit(solution)/shard_map/deliver/pallas_call | solution.py:442
where the time goes:
time: 25.5 us; the launch traced here: 25.3 us
  Pallas kernels  24.7 us (97%)
  between operations  0.64 us (3%)
    pallas_call x1, Pallas kernels, on_device(): pl.pallas_call(functools.partial(window_kernel, devices), out_shape=shape...  23.6 us
    pallas_call x1, Pallas kernels, on_device(): pl.pallas_call(deliver_kernel, out_shape=shapes, in_specs=[vmem] * 5, out...  1.07 us

commit v1 on v0

v1 whole, which is shorter than its diff:
```python
import functools
import math

import jax
import jax.numpy as jnp
from jax import lax
from jax.experimental import pallas as pl
from jax.experimental.pallas import tpu as pltpu
from jax.sharding import PartitionSpec as P

REACH = 2
EDGE = 8
OUTER, INNER, CENTRE = -1.0 / 12.0, 4.0 / 3.0, -2.5
RCV, SRC, ALT = 0, 1, 2
FIELDS = (RCV, SRC, ALT)
PARTS = 3
MESH = pl.DeviceIdType.MESH


def second(window):
    return (
        OUTER * (window(-2) + window(2)) + INNER * (window(-1) + window(1)) + CENTRE * window(0)
    )


def window_kernel(
    devices,
    src_now_in,
    src_old_in,
    rcv_now_in,
    rcv_old_in,
    medium_in,
    wavelet_in,
    shot_in,
    traces_in,
    rec_x_in,
    lag_order_in,
    src_next,
    src_prior,
    rcv_next,
    rcv_prior,
    board,
    src_old,
    rcv_old,
    medium,
    wavelet,
    shot,
    traces,
    rec_x,
    lag_order,
    padded,
    staged,
    landed,
    levels,
    partial,
    surface,
    spot,
    spot_alt,
    out_send,
    out_recv,
    halo_send,
    halo_recv,
    load_sems,
):
    me = lax.axis_index("wide")
    slab, cells, cells_z = src_old.shape
    steps = wavelet.shape[0]
    rows = 2 * PARTS * slab
    block = slab * rows
    inside = pl.ds(EDGE, cells)
    own_planes = pl.ds(REACH, slab)

    lags = lag_order.shape[0]
    half = (lags - 1) // 2
    middle = devices // 2
    far_first = sorted(range(1, devices), key=lambda distance: abs(distance - middle))

    loads = []
    for index, (source, target) in enumerate(
        (
            (src_now_in, levels.at[0, ALT, own_planes, inside]),
            (src_old_in, src_old),
            (medium_in, medium),
            (rcv_now_in, levels.at[0, RCV, own_planes, inside]),
            (shot_in, shot),
            (traces_in, traces),
            (rec_x_in, rec_x),
            (rcv_old_in, rcv_old),
            (wavelet_in, wavelet),
            (lag_order_in, lag_order),
        )
    ):
        loads.append(pltpu.make_async_copy(source, target, load_sems.at[index]))
    for load in loads[:3]:
        load.start()

    barrier = pltpu.get_barrier_semaphore()
    for distance in far_first:
        pl.semaphore_signal(
            barrier,
            inc=1,
            device_id={"wide": lax.rem(me + distance, devices)},
            device_id_type=MESH,
        )
    for load in loads[3:]:
        load.start()

    zero_edge = jnp.zeros((EDGE, cells_z), jnp.float32)
    zero_plane = jnp.zeros((cells, cells_z), jnp.float32)
    zero_half = jnp.zeros((half, cells_z), jnp.float32)
    for level in range(steps):
        for field in FIELDS:
            for at in range(REACH, REACH + slab):
                levels[level, field, at, 0:EDGE, :] = zero_edge
                levels[level, field, at, EDGE + cells : EDGE + cells + EDGE, :] = zero_edge

    row_at = lax.broadcasted_iota(jnp.int32, (cells, cells_z), 0)
    lane_at = lax.broadcasted_iota(jnp.int32, (cells, cells_z), 1)

    def along_rows(field, level, at):
        centre = levels[level, field, REACH + at, inside, :]

        def window(shift):
            if shift == 0:
                return centre
            return levels[level, field, REACH + at, pl.ds(EDGE + shift, cells), :]

        return second(window)

    for load in loads[:3]:
        load.wait()
    for at in range(slab):
        sent_rows = (
            lambda: levels[0, ALT, REACH + at, inside, :],
            lambda: src_old[at],
            lambda: along_rows(ALT, 0, at),
        )
        for part, rows_of in enumerate(sent_rows):
            partial[0, 0] = rows_of()
            for y in range(slab):
                into = at * rows + part * slab + y
                staged[pl.ds(into, devices, stride=block), :] = partial[
                    0, 0, pl.ds(y, devices, stride=slab), :
                ]
        for part in range(PARTS):
            for x in range(slab):
                into = at * rows + (PARTS + part) * slab + x
                staged[pl.ds(into, devices, stride=block), :] = medium[
                    part, at, pl.ds(x, devices, stride=slab), :
                ]

    pl.semaphore_wait(barrier, devices - 1)

    def out_copy(peer):
        return pltpu.make_async_remote_copy(
            src_ref=staged.at[pl.ds(pl.multiple_of(peer * block, 8), block)],
            dst_ref=landed.at[pl.ds(pl.multiple_of(me * block, 8), block)],
            send_sem=out_send,
            recv_sem=out_recv,
            device_id={"wide": peer},
            device_id_type=MESH,
        )

    def halo_copy(field, level, side):
        first = slab if side == 0 else REACH
        source = levels.at[level, field, pl.ds(first, REACH), inside]
        into = 0 if side == 0 else REACH + slab
        peer = me + 1 if side == 0 else me - 1
        return pltpu.make_async_remote_copy(
            src_ref=source,
            dst_ref=levels.at[level, field, pl.ds(into, REACH), inside],
            send_sem=halo_send.at[field, level, side],
            recv_sem=halo_recv.at[field, level, side],
            device_id={"wide": peer},
            device_id_type=MESH,
        )

    def each_side(act):
        @pl.when(me < devices - 1)
        def _():
            act(0)

        @pl.when(me > 0)
        def _():
            act(1)

    def send_halo(field, level):
        each_side(lambda side: halo_copy(field, level, side).start())

    def wait_halo(field, level):
        each_side(lambda side: halo_copy(field, level, 1 - side).wait_recv())

    def wait_sent(field, level):
        each_side(lambda side: halo_copy(field, level, side).wait_send())

    for distance in far_first:
        out_copy(lax.rem(me + distance, devices)).start()

    for load in loads[3:]:
        load.wait()
    send_halo(RCV, 0)
    send_halo(ALT, 0)

    own = pl.ds(pl.multiple_of(me * block, 8), block)
    landed[own, :] = staged[own, :]

    for snap in range(padded.shape[0]):
        for field in (RCV, SRC):
            for y in range(slab):
                padded[snap, field, y, 0:half, :] = zero_half
                padded[snap, field, y, half + cells : 2 * half + cells, :] = zero_half

    @pl.when(me == 0)
    def _():
        for level in range(steps):
            for field in FIELDS:
                for at in range(REACH):
                    levels[level, field, at, inside, :] = zero_plane

    @pl.when(me == devices - 1)
    def _():
        for level in range(steps):
            for field in FIELDS:
                for at in range(REACH):
                    levels[level, field, REACH + slab + at, inside, :] = zero_plane

    deep = lane_at == shot[2]
    column = ((row_at == shot[0]) & deep).astype(jnp.float32)
    column_alt = ((row_at == shot[1]) & deep).astype(jnp.float32)
    for at in range(slab):
        spot[at] = column * (me * slab + at == shot[1]).astype(jnp.float32)
        spot_alt[at] = column_alt * (me * slab + at == shot[0]).astype(jnp.float32)
    x_at = lax.broadcasted_iota(jnp.int32, (cells, traces.shape[2]), 0)
    for y in range(slab):
        onehot = (x_at == rec_x[y : y + 1, :]).astype(jnp.float32)
        for step in range(steps):
            total = jnp.sum(onehot * traces[y, step : step + 1, :], axis=1, keepdims=True)
            surface[step, y] = jnp.where(lane_at == 0, total, 0.0)

    def arrived_rows(part, at):
        return landed[pl.ds(part * slab + at, cells, stride=rows), :]

    def older(field, level, at):
        if level > 0:
            return levels[level - 1, field, REACH + at, inside, :]
        if field == RCV:
            return rcv_old[at]
        if field == ALT:
            return src_old[at]
        return arrived_rows(1, at)

    def speeds(field, at):
        if field == ALT:
            return tuple(arrived_rows(PARTS + part, at) for part in (0, 1, 2))
        return tuple(medium[part, at] for part in (1, 0, 2))

    def local(field, level):
        for at in range(slab):
            centre = levels[level, field, REACH + at, inside, :]
            _, rows_speed, lanes_speed = speeds(field, at)

            def along_lanes(shift):
                if shift == 0:
                    return centre
                turned = pltpu.roll(centre, (-shift) % cells_z, 1)
                kept = lane_at >= -shift if shift < 0 else lane_at < cells_z - shift
                return jnp.where(kept, turned, 0.0)

            partial[field, at] = (
                2.0 * centre
                - older(field, level, at)
                + rows_speed * along_rows(field, level, at)
                + lanes_speed * second(along_lanes)
            )

    def finish(field, level):
        for at in range(slab):
            def along_planes(shift):
                return levels[level, field, REACH + at + shift, inside, :]

            if field == SRC and level == 0:
                bend = arrived_rows(2, at)
            else:
                bend = second(along_planes)
            if field == RCV:
                added = surface[level, at]
            else:
                added = -wavelet[level] * (spot if field == SRC else spot_alt)[at]
            levels[level + 1, field, REACH + at, inside, :] = (
                partial[field, at] + speeds(field, at)[0] * bend + added
            )

    def keep(field, level):
        snap = level // 2 - 1
        for y in range(slab):
            padded[snap, field, y, half : half + cells, :] = levels[
                level, field, REACH + y, inside, :
            ]

    def correlate(snap):
        for plane in range(lags):
            slot = lag_order[plane]
            at_src = pl.ds(2 * half - slot, cells)
            at_rcv = pl.ds(slot, cells)
            for y in range(slab):
                product = padded[snap, SRC, y, at_src, :] * padded[snap, RCV, y, at_rcv, :]
                board[plane, y] = product if snap == 0 else board[plane, y] + product

    local(RCV, 0)
    wait_halo(RCV, 0)
    finish(RCV, 0)
    send_halo(RCV, 1)
    local(RCV, 1)
    wait_halo(ALT, 0)

    arrived = landed.at[pl.ds(0, (devices - 1) * block)]
    pltpu.make_async_copy(arrived, arrived, out_recv).wait()
    for y in range(slab):
        levels[0, SRC, REACH + y, inside, :] = arrived_rows(0, y)
    for field in (ALT, SRC):
        local(field, 0)
        finish(field, 0)
        send_halo(field, 1)
    for level in range(1, steps):
        local(ALT, level)
        local(SRC, level)
        if level == steps - 1:
            keep(SRC, 2)
            keep(RCV, 2)
            correlate(0)
        wait_halo(RCV, level)
        finish(RCV, level)
        if level + 1 < steps:
            send_halo(RCV, level + 1)
            local(RCV, level + 1)
        for field in (ALT, SRC):
            wait_halo(field, level)
            finish(field, level)
            if level + 1 < steps:
                send_halo(field, level + 1)

    keep(SRC, steps)
    keep(RCV, steps)
    correlate(1)
    for at in range(slab):
        src_next[at] = levels[steps, ALT, REACH + at, inside, :]
        src_prior[at] = levels[steps - 1, ALT, REACH + at, inside, :]
        rcv_next[at] = levels[steps, RCV, REACH + at, inside, :]
        rcv_prior[at] = levels[steps - 1, RCV, REACH + at, inside, :]

    sent = staged.at[pl.ds(0, (devices - 1) * block)]
    pltpu.make_async_copy(sent, sent, out_send).wait()
    for level in range(steps):
        for field in FIELDS:
            if level > 0 or field != SRC:
                wait_sent(field, level)


def deliver_kernel(*refs):
    count = (len(refs) - 1) // 2
    copies = [
        pltpu.make_async_copy(refs[i], refs[count + i], refs[-1].at[i]) for i in range(count)
    ]
    for copy in copies:
        copy.start()
    for copy in copies:
        copy.wait()


def solution(mesh):
    devices = mesh.shape["wide"]

    def on_device(
        src_now, src_old, rcv_now, rcv_old, medium, wavelet, shot, traces, rec_x, lag_order
    ):
        slab, cells, cells_z = src_now.shape
        assert rcv_now.shape == (slab, cells_z, cells) and slab >= REACH
        assert slab * devices == cells
        steps = wavelet.shape[0]
        lags = lag_order.shape[0]
        half = (lags - 1) // 2
        span = slab + 2 * REACH
        rows = 2 * PARTS * slab
        f32 = jnp.float32
        vmem = pl.BlockSpec(memory_space=pltpu.VMEM)
        hbm = pl.BlockSpec(memory_space=pltpu.HBM)
        field_shape = jax.ShapeDtypeStruct((slab, cells, cells_z), f32)
        board_shape = jax.ShapeDtypeStruct((lags, slab, cells, cells_z), f32)
        shapes = (field_shape,) * 4 + (board_shape,)
        taken = steps // 2
        turn = lambda array: jnp.swapaxes(array, -1, -2)
        like = lambda array: pltpu.VMEM(array.shape, array.dtype)
        scalars = lambda array: pltpu.SMEM(array.shape, array.dtype)
        rcv_now, rcv_old, medium, traces = map(turn, (rcv_now, rcv_old, medium, traces))
        scratch = [
            like(src_old),
            like(rcv_old),
            like(medium),
            scalars(wavelet),
            scalars(shot),
            like(traces),
            like(rec_x),
            scalars(lag_order),
            pltpu.VMEM((taken, 2, slab, cells + 2 * half, cells_z), f32),
            pltpu.VMEM((cells * rows, cells_z), f32),
            pltpu.VMEM((cells * rows, cells_z), f32),
            pltpu.VMEM((steps + 1, 3, span, cells + 2 * EDGE, cells_z), f32),
            pltpu.VMEM((3, slab, cells, cells_z), f32),
            pltpu.VMEM((steps, slab, cells, cells_z), f32),
            pltpu.VMEM((slab, cells, cells_z), f32),
            pltpu.VMEM((slab, cells, cells_z), f32),
        ]
        held = sum(4 * math.prod(each.shape) for each in scratch + list(shapes))
        results = pl.pallas_call(
            functools.partial(window_kernel, devices),
            out_shape=shapes,
            in_specs=[hbm] * 10,
            out_specs=(vmem,) * 5,
            scratch_shapes=scratch
            + [pltpu.SemaphoreType.DMA] * 2
            + [
                pltpu.SemaphoreType.DMA((3, steps, 2)),
                pltpu.SemaphoreType.DMA((3, steps, 2)),
                pltpu.SemaphoreType.DMA((10,)),
            ],
            compiler_params=pltpu.CompilerParams(
                collective_id=0, has_side_effects=True, vmem_limit_bytes=held + (4 << 20)
            ),
            name="window",
        )(
            *(
                pltpu.with_memory_space_constraint(array, pltpu.HBM)
                for array in (
                    src_now,
                    src_old,
                    rcv_now,
                    rcv_old,
                    medium,
                    wavelet,
                    shot,
                    traces,
                    rec_x,
                    lag_order,
                )
            )
        )
        outs = pl.pallas_call(
            deliver_kernel,
            out_shape=shapes,
            in_specs=[vmem] * 5,
            out_specs=(hbm,) * 5,
            scratch_shapes=[pltpu.SemaphoreType.DMA((5,))],
            compiler_params=pltpu.CompilerParams(vmem_limit_bytes=held + (4 << 20)),
            name="deliver",
        )(*results)
        return outs[0], outs[1], turn(outs[2]), turn(outs[3]), turn(outs[4])

    return jax.shard_map(
        on_device,
        mesh=mesh,
        in_specs=(
            P("wide", "shots", None),
            P("wide", "shots", None),
            P("wide", "shots", None),
            P("wide", "shots", None),
            P(None, "wide", None, None),
            P(),
            P("shots"),
            P("wide", "shots", None),
            P("wide", "shots"),
            P(),
        ),
        out_specs=(
            P("wide", "shots", None),
            P("wide", "shots", None),
            P("wide", "shots", None),
            P("wide", "shots", None),
            P("shots", "wide", None, None),
        ),
        check_vma=False,
    )
```

time: 25.5 us -> 22.4 us (0.88)
  the two profiles are of different devices: /device:TPU:0 before, /device:TPU:3 now
where the time goes in v1:
time: 22.4 us; the launch traced here: 22.2 us
  Pallas kernels  21.6 us (96%)
  between operations  0.64 us (3%)
    pallas_call x1, Pallas kernels, on_device(): pl.pallas_call(functools.partial(window_kernel, devices), out_shape=shape...  20.5 us
    pallas_call x1, Pallas kernels, on_device(): pl.pallas_call(deliver_kernel, out_shape=shapes, in_specs=[vmem] * 5, out...  1.07 us

profile of v1, /device:TPU:3, one launch (start us, length us, event | category | flops | bytes accessed | tf_op | source)
XLA Modules:
  0.0 22.2 jit_solution(18302886255609773196)
XLA Ops:
  0.6 20.5 %window.1 = (f32[2,32,128]{2,1,0:T(8,128)S(1)}, f32[2,32,128]{2,1,0:T(8,128)S(1)}, f32[2,32,128]{2,1,0:T(8,128)S(1)}, f32[2,32,128]{2,1,0:T(8,128)S(1)}, f32[33,2,32,128]{3,2,1,0:T(8,128)S(1)}) custom-call(f32[2,32,128]{2,1,0:T(8,128)} %src_now_in.1, f32[2,32,128]{2,1,0:T(8,128)} %src_old_in.1, f32[2,32,128]{2,1,0:T(8,128)} %bitcast.8, ...), custom_call_target="tpu_custom_call" | custom-call | tf_op jit(solution)/shard_map/window/pallas_call | solution.py:414
  21.2 1.1 %deliver.1 = (f32[2,32,128]{2,1,0:T(8,128)}, f32[2,32,128]{2,1,0:T(8,128)}, f32[2,32,128]{2,1,0:T(8,128)}, f32[2,32,128]{2,1,0:T(8,128)}, f32[33,2,32,128]{3,2,1,0:T(8,128)}) custom-call(f32[2,32,128]{2,1,0:T(8,128)S(1)} %get-tuple-element.15.refs_0_, f32[2,32,128]{2,1,0:T(8,128)S(1)} %get-tuple-element.16.refs_1_, ...), custom_call_target="tpu_custom_call" | custom-call | tf_op jit(solution)/shard_map/deliver/pallas_call | solution.py:447

commit v2 on v1

v2 whole, which is shorter than its diff:
```python
import functools
import math

import jax
import jax.numpy as jnp
from jax import lax
from jax.experimental import pallas as pl
from jax.experimental.pallas import tpu as pltpu
from jax.sharding import PartitionSpec as P

REACH = 2
EDGE = 8
OUTER, INNER, CENTRE = -1.0 / 12.0, 4.0 / 3.0, -2.5
SRC, ALT = 0, 1
FIELDS = (SRC, ALT)
PARTS = 3
LEFT, RIGHT = 0, 1
MESH = pl.DeviceIdType.MESH


def second(window):
    return (
        OUTER * (window(-2) + window(2)) + INNER * (window(-1) + window(1)) + CENTRE * window(0)
    )


def window_kernel(
    devices,
    src_now_in,
    src_old_in,
    rcv_now_in,
    rcv_old_in,
    medium_in,
    wavelet_in,
    shot_in,
    traces_in,
    rec_x_in,
    lag_order_in,
    src_next,
    src_prior,
    rcv_next,
    rcv_prior,
    board,
    src_old,
    rcv_old,
    medium,
    medium_alt,
    wavelet,
    shot,
    traces,
    rec_x,
    lag_order,
    padded,
    staged,
    landed,
    waves,
    echoes,
    partial,
    partial_rcv,
    surface,
    columns,
    out_send,
    out_recv,
    halo_send,
    halo_recv,
    echo_send,
    echo_recv,
    pair_send,
    pair_recv,
    load_sems,
):
    me = lax.axis_index("wide")
    pairs = devices // 2
    pair = me // 2
    odd = lax.rem(me, 2)
    slab, cells, cells_z = rcv_old.shape
    both = 2 * slab
    steps = wavelet.shape[0]
    last = steps - 1
    rows = 2 * PARTS * both
    block = slab * rows
    inside = pl.ds(EDGE, cells)
    mine = pl.ds(odd * slab, slab)
    mine_waves = pl.ds(REACH + odd * slab, slab)
    own_echoes = pl.ds(REACH, slab)

    lags = lag_order.shape[0]
    half = (lags - 1) // 2
    far_first = sorted(range(1, devices), key=lambda distance: abs(distance - devices // 2))
    far_pairs = sorted(range(1, pairs), key=lambda distance: abs(distance - pairs // 2))

    def when_first(act):
        pl.when(odd == 0)(act)

    def when_second(act):
        pl.when(odd == 1)(act)

    loads = []
    for index, (source, target) in enumerate(
        (
            (src_now_in, waves.at[0, ALT, mine_waves, inside]),
            (src_old_in, src_old.at[mine]),
            (medium_in, medium.at[:, mine]),
            (rcv_now_in, echoes.at[0, own_echoes, inside]),
            (shot_in, shot),
            (traces_in, traces),
            (rec_x_in, rec_x),
            (rcv_old_in, rcv_old),
            (wavelet_in, wavelet),
            (lag_order_in, lag_order),
        )
    ):
        loads.append(pltpu.make_async_copy(source, target, load_sems.at[index]))
    for load in loads[:3]:
        load.start()

    barrier = pltpu.get_barrier_semaphore()

    def greet(peer):
        pl.semaphore_signal(
            barrier, inc=1, device_id={"wide": peer}, device_id_type=MESH
        )

    @when_second
    def _():
        for distance in far_first:
            greet(lax.rem(me + distance, devices))

    @when_first
    def _():
        greet(me + 1)
        pl.when(pair > 0)(lambda: greet(me - 1))

    for load in loads[3:]:
        load.start()

    zero_edge = jnp.zeros((EDGE, cells_z), jnp.float32)
    zero_plane = jnp.zeros((cells, cells_z), jnp.float32)
    zero_half = jnp.zeros((half, cells_z), jnp.float32)

    for field in FIELDS:
        for level in range(steps):
            for at in range(REACH, REACH + both):
                waves[level, field, at, 0:EDGE, :] = zero_edge
                waves[level, field, at, EDGE + cells : EDGE + cells + EDGE, :] = zero_edge
    for level in range(steps):
        for at in range(REACH, REACH + slab):
            echoes[level, at, 0:EDGE, :] = zero_edge
            echoes[level, at, EDGE + cells : EDGE + cells + EDGE, :] = zero_edge

    row_at = lax.broadcasted_iota(jnp.int32, (cells, cells_z), 0)
    lane_at = lax.broadcasted_iota(jnp.int32, (cells, cells_z), 1)

    def along_rows(plane):
        def window(shift):
            return plane(pl.ds(EDGE + shift, cells))

        return second(window)

    for load in loads[:3]:
        load.wait()
    for at in range(slab):
        def now_rows(where):
            return waves[0, ALT, REACH + odd * slab + at, where, :]

        sent_rows = (
            lambda: now_rows(inside),
            lambda: src_old[odd * slab + at],
            lambda: along_rows(now_rows),
        )
        for part, rows_of in enumerate(sent_rows):
            partial[part, at] = rows_of()
            for y in range(both):
                into = at * rows + part * both + y
                staged[pl.ds(into, pairs, stride=block), :] = partial[
                    part, at, pl.ds(y, pairs, stride=both), :
                ]
        for part in range(PARTS):
            for x in range(both):
                into = at * rows + (PARTS + part) * both + x
                staged[pl.ds(into, pairs, stride=block), :] = medium[
                    part, odd * slab + at, pl.ds(x, pairs, stride=both), :
                ]

    pl.semaphore_wait(barrier, pairs + odd * (pair < pairs - 1).astype(jnp.int32))

    def remote(source, target, send, recv, peer):
        return pltpu.make_async_remote_copy(
            src_ref=source,
            dst_ref=target,
            send_sem=send,
            recv_sem=recv,
            device_id={"wide": peer},
            device_id_type=MESH,
        )

    def out_copy(to):
        return remote(
            staged.at[pl.ds(pl.multiple_of(to * block, 8), block)],
            landed.at[pl.ds(pl.multiple_of(me * block, 8), block)],
            out_send,
            out_recv,
            2 * to + 1,
        )

    def pair_copy(index):
        early = index < 3
        source = (
            waves.at[0, ALT, pl.ds(REACH, slab), inside],
            src_old.at[pl.ds(0, slab)],
            medium.at[:, pl.ds(0, slab)],
            medium_alt.at[:, pl.ds(0, slab)],
            waves.at[last - 1, :, pl.ds(REACH, slab), inside],
            waves.at[last, :, pl.ds(REACH, both), inside],
        )[index]
        peer = 2 * pair + 1 if early else 2 * pair
        return remote(source, source, pair_send.at[index], pair_recv.at[index], peer)

    def halo_copy(field, level, side):
        first = both if side == LEFT else REACH
        into = 0 if side == LEFT else REACH + both
        to = pair + 1 if side == LEFT else pair - 1
        peer = 2 * to if level == last and side == LEFT else 2 * to + 1
        return remote(
            waves.at[level, field, pl.ds(first, REACH), inside],
            waves.at[level, field, pl.ds(into, REACH), inside],
            halo_send.at[field, level, side],
            halo_recv.at[field, level, side],
            peer,
        )

    def sends_to(side):
        return pair < pairs - 1 if side == LEFT else pair > 0

    def gets_from(side):
        return pair > 0 if side == LEFT else pair < pairs - 1

    def send_halo(field, level, side):
        pl.when(sends_to(side))(lambda: halo_copy(field, level, side).start())

    def wait_sent(field, level, side):
        pl.when(sends_to(side))(lambda: halo_copy(field, level, side).wait_send())

    def wait_halo(field, level, side):
        pl.when(gets_from(side))(lambda: halo_copy(field, level, side).wait_recv())

    def echo_copy(level, side):
        first = slab if side == LEFT else REACH
        into = 0 if side == LEFT else REACH + slab
        return remote(
            echoes.at[level, pl.ds(first, REACH), inside],
            echoes.at[level, pl.ds(into, REACH), inside],
            echo_send.at[level, side],
            echo_recv.at[level, side],
            me + 1 if side == LEFT else me - 1,
        )

    def each_side(act):
        pl.when(me < devices - 1)(lambda: act(LEFT))
        pl.when(me > 0)(lambda: act(RIGHT))

    def send_echo(level):
        each_side(lambda side: echo_copy(level, side).start())

    def wait_echo(level):
        each_side(lambda side: echo_copy(level, 1 - side).wait_recv())

    loads[3].wait()
    send_echo(0)

    for distance in far_pairs:
        out_copy(lax.rem(pair + distance, pairs)).start()

    for load in loads[4:]:
        load.wait()

    @when_first
    def _():
        out_copy(pair).start()
        send_halo(ALT, 0, RIGHT)
        for index in range(3):
            pair_copy(index).start()

    @when_second
    def _():
        send_halo(ALT, 0, LEFT)
        own = pl.ds(pl.multiple_of(me * block, 8), block)
        landed[own, :] = staged[pl.ds(pl.multiple_of(pair * block, 8), block), :]


    for snap in range(padded.shape[0]):
        for field in range(2):
            for y in range(slab):
                padded[snap, field, y, 0:half, :] = zero_half
                padded[snap, field, y, half + cells : 2 * half + cells, :] = zero_half

    def clear_planes(first):
        for level in range(steps):
            for field in FIELDS:
                for at in range(REACH):
                    waves[level, field, first + at, inside, :] = zero_plane

    pl.when(pair == 0)(lambda: clear_planes(0))
    pl.when(pair == pairs - 1)(lambda: clear_planes(REACH + both))

    def clear_echoes(first):
        for level in range(steps):
            for at in range(REACH):
                echoes[level, first + at, inside, :] = zero_plane

    pl.when(me == 0)(lambda: clear_echoes(0))
    pl.when(me == devices - 1)(lambda: clear_echoes(REACH + slab))

    deep = lane_at == shot[2]
    columns[SRC] = ((row_at == shot[0]) & deep).astype(jnp.float32)
    columns[ALT] = ((row_at == shot[1]) & deep).astype(jnp.float32)
    x_at = lax.broadcasted_iota(jnp.int32, (cells, traces.shape[2]), 0)
    for y in range(slab):
        onehot = (x_at == rec_x[y : y + 1, :]).astype(jnp.float32)
        for step in range(steps):
            total = jnp.sum(onehot * traces[y, step : step + 1, :], axis=1, keepdims=True)
            surface[step, y] = jnp.where(lane_at == 0, total, 0.0)

    def arrived_rows(part, at):
        return landed[pl.ds(part * both + at, cells, stride=rows), :]

    def along_lanes(centre):
        def window(shift):
            if shift == 0:
                return centre
            turned = pltpu.roll(centre, (-shift) % cells_z, 1)
            kept = lane_at >= -shift if shift < 0 else lane_at < cells_z - shift
            return jnp.where(kept, turned, 0.0)

        return second(window)

    def flat(plane, older, rows_speed, lanes_speed):
        centre = plane(inside)
        return (
            2.0 * centre
            - older
            + rows_speed * along_rows(plane)
            + lanes_speed * along_lanes(centre)
        )

    def speed(field, part, at):
        if field == ALT:
            return medium_alt[part, at]
        return medium[(1, 0, 2)[part], at]

    def local(field, level, ats):
        for at in ats:
            def plane(where):
                return waves[level, field, REACH + at, where, :]

            if level > 0:
                older = waves[level - 1, field, REACH + at, inside, :]
            elif field == ALT:
                older = src_old[at]
            else:
                older = arrived_rows(1, at)
            partial[field, at] = flat(plane, older, speed(field, 1, at), speed(field, 2, at))

    def finish(field, level, ats):
        for at in ats:
            def along_planes(shift):
                return waves[level, field, REACH + at + shift, inside, :]

            if field == SRC and level == 0:
                bend = arrived_rows(2, at)
            else:
                bend = second(along_planes)
            hit = (pair * both + at == shot[1 if field == SRC else 0]).astype(jnp.float32)
            waves[level + 1, field, REACH + at, inside, :] = (
                partial[field, at]
                + speed(field, 0, at) * bend
                - (wavelet[level] * hit) * columns[field]
            )

    def local_both(level, ats):
        for field in FIELDS:
            local(field, level, ats)

    def local_rcv(level):
        for at in range(slab):
            def plane(where):
                return echoes[level, REACH + at, where, :]

            older = echoes[level - 1, REACH + at, inside, :] if level > 0 else rcv_old[at]
            here = odd * slab + at
            partial_rcv[at] = flat(plane, older, medium[0, here], medium[2, here])

    def finish_rcv(level):
        for at in range(slab):
            def along_planes(shift):
                return echoes[level, REACH + at + shift, inside, :]

            echoes[level + 1, REACH + at, inside, :] = (
                partial_rcv[at]
                + medium[1, odd * slab + at] * second(along_planes)
                + surface[level, at]
            )

    def keep_src(level):
        for y in range(slab):
            padded[level // 2 - 1, 0, y, half : half + cells, :] = waves[
                level, SRC, REACH + odd * slab + y, inside, :
            ]

    def keep_rcv(level):
        for y in range(slab):
            padded[level // 2 - 1, 1, y, half : half + cells, :] = echoes[
                level, REACH + y, inside, :
            ]

    def correlate(snap):
        for plane in range(lags):
            slot = lag_order[plane]
            at_src = pl.ds(2 * half - slot, cells)
            at_rcv = pl.ds(slot, cells)
            for y in range(slab):
                product = padded[snap, 0, y, at_src, :] * padded[snap, 1, y, at_rcv, :]
                board[plane, y] = product if snap == 0 else board[plane, y] + product

    everyone = range(both)
    firsts, seconds = range(slab), range(slab, both)

    def advance_rcv(level):
        wait_echo(level)
        finish_rcv(level)
        if level < last:
            send_echo(level + 1)
            local_rcv(level + 1)

    local_rcv(0)
    advance_rcv(0)

    @when_second
    def _():
        for index in range(3):
            pair_copy(index).wait_recv()
        for side in (LEFT, RIGHT):
            wait_halo(ALT, 0, side)
        arrived = landed.at[pl.ds(0, (devices - 1) * block)]
        pltpu.make_async_copy(arrived, arrived, out_recv).wait()
        for at in everyone:
            waves[0, SRC, REACH + at, inside, :] = arrived_rows(0, at)
        for field in FIELDS:
            if field == ALT:
                for at in everyone:
                    for part in range(PARTS):
                        medium_alt[part, at] = arrived_rows(PARTS + part, at)
            local(field, 0, everyone)
            finish(field, 0, everyone)
            for side in (RIGHT, LEFT):
                send_halo(field, 1, side)
        pair_copy(3).start()
        local_both(1, everyone)
        for field in FIELDS:
            for side in (LEFT, RIGHT):
                wait_sent(field, 1, side)

    advance_rcv(1)
    for level in range(1, last):

        @when_second
        def _():
            for field in FIELDS:
                for side in (LEFT, RIGHT):
                    wait_halo(field, level, side)
                finish(field, level, everyone)
                for side in (RIGHT, LEFT):
                    send_halo(field, level + 1, side)
            if level + 1 == last - 1:
                pair_copy(4).start()
            if level + 1 == last:
                pair_copy(5).start()
            local_both(level + 1, everyone if level + 1 < last else seconds)
            for field in FIELDS:
                for side in (LEFT, RIGHT):
                    wait_sent(field, level + 1, side)

        advance_rcv(level + 1)

    @when_first
    def _():
        for index in (3, 4):
            pair_copy(index).wait_recv()

    keep_src(2)
    keep_rcv(2)
    keep_rcv(steps)
    correlate(0)
    for at in range(slab):
        rcv_next[at] = echoes[steps, REACH + at, inside, :]
        rcv_prior[at] = echoes[last, REACH + at, inside, :]

    @when_first
    def _():
        pair_copy(5).wait_recv()
        local_both(last, firsts)

    def arrive(field):
        @when_second
        def _():
            wait_halo(field, last, RIGHT)
            finish(field, last, seconds)

        @when_first
        def _():
            wait_halo(field, last, LEFT)
            finish(field, last, firsts)

    arrive(SRC)
    keep_src(steps)
    correlate(1)
    arrive(ALT)
    for at in range(slab):
        src_next[at] = waves[steps, ALT, REACH + odd * slab + at, inside, :]
        src_prior[at] = waves[last, ALT, REACH + odd * slab + at, inside, :]

    @when_first
    def _():
        sent = staged.at[pl.ds(0, pairs * block)]
        pltpu.make_async_copy(sent, sent, out_send).wait()
        wait_sent(ALT, 0, RIGHT)
        for index in range(3):
            pair_copy(index).wait_send()

    @when_second
    def _():
        sent = staged.at[pl.ds(0, (pairs - 1) * block)]
        pltpu.make_async_copy(sent, sent, out_send).wait()
        wait_sent(ALT, 0, LEFT)
        for index in range(3, 6):
            pair_copy(index).wait_send()

    for level in range(steps):
        each_side(lambda side: echo_copy(level, side).wait_send())


def deliver_kernel(*refs):
    count = (len(refs) - 1) // 2
    copies = [
        pltpu.make_async_copy(refs[i], refs[count + i], refs[-1].at[i]) for i in range(count)
    ]
    for copy in copies:
        copy.start()
    for copy in copies:
        copy.wait()


def solution(mesh):
    devices = mesh.shape["wide"]

    def on_device(
        src_now, src_old, rcv_now, rcv_old, medium, wavelet, shot, traces, rec_x, lag_order
    ):
        slab, cells, cells_z = src_now.shape
        assert rcv_now.shape == (slab, cells_z, cells) and slab >= REACH
        assert slab * devices == cells and devices % 2 == 0
        steps = wavelet.shape[0]
        lags = lag_order.shape[0]
        half = (lags - 1) // 2
        rows = 4 * PARTS * slab
        f32 = jnp.float32
        vmem = pl.BlockSpec(memory_space=pltpu.VMEM)
        hbm = pl.BlockSpec(memory_space=pltpu.HBM)
        field_shape = jax.ShapeDtypeStruct((slab, cells, cells_z), f32)
        board_shape = jax.ShapeDtypeStruct((lags, slab, cells, cells_z), f32)
        shapes = (field_shape,) * 4 + (board_shape,)
        taken = steps // 2
        turn = lambda array: jnp.swapaxes(array, -1, -2)
        like = lambda array: pltpu.VMEM(array.shape, array.dtype)
        scalars = lambda array: pltpu.SMEM(array.shape, array.dtype)
        rcv_now, rcv_old, medium, traces = map(turn, (rcv_now, rcv_old, medium, traces))
        both = 2 * slab
        field = lambda *lead: pltpu.VMEM((*lead, cells, cells_z), f32)
        wide = lambda *lead: pltpu.VMEM((*lead, cells + 2 * EDGE, cells_z), f32)
        scratch = [
            field(both),
            like(rcv_old),
            field(PARTS, both),
            field(PARTS, both),
            scalars(wavelet),
            scalars(shot),
            like(traces),
            like(rec_x),
            scalars(lag_order),
            pltpu.VMEM((taken, 2, slab, cells + 2 * half, cells_z), f32),
            pltpu.VMEM((devices // 2 * slab * rows, cells_z), f32),
            pltpu.VMEM((devices * slab * rows, cells_z), f32),
            wide(steps + 1, 2, both + 2 * REACH),
            wide(steps + 1, slab + 2 * REACH),
            field(PARTS, both),
            field(slab),
            field(steps, slab),
            field(2),
        ]
        held = sum(4 * math.prod(each.shape) for each in scratch + list(shapes))
        results = pl.pallas_call(
            functools.partial(window_kernel, devices),
            out_shape=shapes,
            in_specs=[hbm] * 10,
            out_specs=(vmem,) * 5,
            scratch_shapes=scratch
            + [pltpu.SemaphoreType.DMA] * 2
            + [pltpu.SemaphoreType.DMA((2, steps, 2))] * 2
            + [pltpu.SemaphoreType.DMA((steps, 2))] * 2
            + [pltpu.SemaphoreType.DMA((6,))] * 2
            + [pltpu.SemaphoreType.DMA((10,))],
            compiler_params=pltpu.CompilerParams(
                collective_id=0, has_side_effects=True, vmem_limit_bytes=held + (4 << 20)
            ),
            name="window",
        )(
            *(
                pltpu.with_memory_space_constraint(array, pltpu.HBM)
                for array in (
                    src_now,
                    src_old,
                    rcv_now,
                    rcv_old,
                    medium,
                    wavelet,
                    shot,
                    traces,
                    rec_x,
                    lag_order,
                )
            )
        )
        outs = pl.pallas_call(
            deliver_kernel,
            out_shape=shapes,
            in_specs=[vmem] * 5,
            out_specs=(hbm,) * 5,
            scratch_shapes=[pltpu.SemaphoreType.DMA((5,))],
            compiler_params=pltpu.CompilerParams(vmem_limit_bytes=held + (4 << 20)),
            name="deliver",
        )(*results)
        return outs[0], outs[1], turn(outs[2]), turn(outs[3]), turn(outs[4])

    return jax.shard_map(
        on_device,
        mesh=mesh,
        in_specs=(
            P("wide", "shots", None),
            P("wide", "shots", None),
            P("wide", "shots", None),
            P("wide", "shots", None),
            P(None, "wide", None, None),
            P(),
            P("shots"),
            P("wide", "shots", None),
            P("wide", "shots"),
            P(),
        ),
        out_specs=(
            P("wide", "shots", None),
            P("wide", "shots", None),
            P("wide", "shots", None),
            P("wide", "shots", None),
            P("shots", "wide", None, None),
        ),
        check_vma=False,
    )
```

time: 22.4 us -> 21.7 us (0.969)
  the two profiles are of different devices: /device:TPU:3 before, /device:TPU:1 now
where the time goes in v2:
time: 21.7 us; the launch traced here: 21.6 us
  Pallas kernels  20.9 us (96%)
  between operations  0.64 us (3%)
    pallas_call x1, Pallas kernels, on_device(): pl.pallas_call(functools.partial(window_kernel, devices), out_shape=shape...  19.9 us
    pallas_call x1, Pallas kernels, on_device(): pl.pallas_call(deliver_kernel, out_shape=shapes, in_specs=[vmem] * 5, out...  1.07 us

profile of v2, /device:TPU:1, one launch (start us, length us, event | category | flops | bytes accessed | tf_op | source)
XLA Modules:
  0.0 21.6 jit_solution(17925738706227176007)
XLA Ops:
  0.6 19.9 %window.1 = (f32[2,32,128]{2,1,0:T(8,128)S(1)}, f32[2,32,128]{2,1,0:T(8,128)S(1)}, f32[2,32,128]{2,1,0:T(8,128)S(1)}, f32[2,32,128]{2,1,0:T(8,128)S(1)}, f32[33,2,32,128]{3,2,1,0:T(8,128)S(1)}) custom-call(f32[2,32,128]{2,1,0:T(8,128)} %src_now_in.1, f32[2,32,128]{2,1,0:T(8,128)} %src_old_in.1, f32[2,32,128]{2,1,0:T(8,128)} %bitcast.8, ...), custom_call_target="tpu_custom_call" | custom-call | tf_op jit(solution)/shard_map/window/pallas_call | solution.py:601
  20.5 1.1 %deliver.1 = (f32[2,32,128]{2,1,0:T(8,128)}, f32[2,32,128]{2,1,0:T(8,128)}, f32[2,32,128]{2,1,0:T(8,128)}, f32[2,32,128]{2,1,0:T(8,128)}, f32[33,2,32,128]{3,2,1,0:T(8,128)}) custom-call(f32[2,32,128]{2,1,0:T(8,128)S(1)} %get-tuple-element.15.refs_0_, f32[2,32,128]{2,1,0:T(8,128)S(1)} %get-tuple-element.16.refs_1_, ...), custom_call_target="tpu_custom_call" | custom-call | tf_op jit(solution)/shard_map/deliver/pallas_call | solution.py:633

commit v3 on v2

--- a/solution.py
+++ b/solution.py
@@ -77,7 +77,7 @@
     both = 2 * slab
     steps = wavelet.shape[0]
     last = steps - 1
-    rows = 2 * PARTS * both
+    rows = PARTS * both
     block = slab * rows
     inside = pl.ds(EDGE, cells)
     mine = pl.ds(odd * slab, slab)
@@ -172,13 +172,13 @@
             partial[part, at] = rows_of()
             for y in range(both):
                 into = at * rows + part * both + y
-                staged[pl.ds(into, pairs, stride=block), :] = partial[
+                staged[SRC, pl.ds(into, pairs, stride=block), :] = partial[
                     part, at, pl.ds(y, pairs, stride=both), :
                 ]
         for part in range(PARTS):
             for x in range(both):
-                into = at * rows + (PARTS + part) * both + x
-                staged[pl.ds(into, pairs, stride=block), :] = medium[
+                into = at * rows + part * both + x
+                staged[ALT, pl.ds(into, pairs, stride=block), :] = medium[
                     part, odd * slab + at, pl.ds(x, pairs, stride=both), :
                 ]
 
@@ -194,12 +194,12 @@
             device_id_type=MESH,
         )
 
-    def out_copy(to):
+    def out_copy(field, to):
         return remote(
-            staged.at[pl.ds(pl.multiple_of(to * block, 8), block)],
-            landed.at[pl.ds(pl.multiple_of(me * block, 8), block)],
-            out_send,
-            out_recv,
+            staged.at[field, pl.ds(pl.multiple_of(to * block, 8), block)],
+            landed.at[field, pl.ds(pl.multiple_of(me * block, 8), block)],
+            out_send.at[field],
+            out_recv.at[field],
             2 * to + 1,
         )
 
@@ -268,15 +268,17 @@
     loads[3].wait()
     send_echo(0)
 
-    for distance in far_pairs:
-        out_copy(lax.rem(pair + distance, pairs)).start()
+    for field in FIELDS:
+        for distance in far_pairs:
+            out_copy(field, lax.rem(pair + distance, pairs)).start()
 
     for load in loads[4:]:
         load.wait()
 
     @when_first
     def _():
-        out_copy(pair).start()
+        for field in FIELDS:
+            out_copy(field, pair).start()
         send_halo(ALT, 0, RIGHT)
         for index in range(3):
             pair_copy(index).start()
@@ -285,7 +287,10 @@
     def _():
         send_halo(ALT, 0, LEFT)
         own = pl.ds(pl.multiple_of(me * block, 8), block)
-        landed[own, :] = staged[pl.ds(pl.multiple_of(pair * block, 8), block), :]
+        for field in FIELDS:
+            landed[field, own, :] = staged[
+                field, pl.ds(pl.multiple_of(pair * block, 8), block), :
+            ]
 
 
     for snap in range(padded.shape[0]):
@@ -321,8 +326,8 @@
             total = jnp.sum(onehot * traces[y, step : step + 1, :], axis=1, keepdims=True)
             surface[step, y] = jnp.where(lane_at == 0, total, 0.0)
 
-    def arrived_rows(part, at):
-        return landed[pl.ds(part * both + at, cells, stride=rows), :]
+    def arrived_rows(field, part, at):
+        return landed[field, pl.ds(part * both + at, cells, stride=rows), :]
 
     def along_lanes(centre):
         def window(shift):
@@ -358,7 +363,7 @@
             elif field == ALT:
                 older = src_old[at]
             else:
-                older = arrived_rows(1, at)
+                older = arrived_rows(SRC, 1, at)
             partial[field, at] = flat(plane, older, speed(field, 1, at), speed(field, 2, at))
 
     def finish(field, level, ats):
@@ -367,7 +372,7 @@
                 return waves[level, field, REACH + at + shift, inside, :]
 
             if field == SRC and level == 0:
-                bend = arrived_rows(2, at)
+                bend = arrived_rows(SRC, 2, at)
             else:
                 bend = second(along_planes)
             hit = (pair * both + at == shot[1 if field == SRC else 0]).astype(jnp.float32)
@@ -435,53 +440,65 @@
     local_rcv(0)
     advance_rcv(0)
 
+    def wait_out(field):
+        arrived = landed.at[field, pl.ds(0, (devices - 1) * block)]
+        pltpu.make_async_copy(arrived, arrived, out_recv.at[field]).wait()
+
+    def begin(field):
+        local(field, 0, everyone)
+        finish(field, 0, everyone)
+        for side in (RIGHT, LEFT):
+            send_halo(field, 1, side)
+        local(field, 1, everyone)
+
+    def one_side(field, level, side):
+        wait_halo(field, level, side)
+        finish(field, level, firsts if side == LEFT else seconds)
+        send_halo(field, level + 1, 1 - side)
+
+    def go_on(field, level):
+        for side in (LEFT, RIGHT):
+            one_side(field, level, side)
+        local(field, level + 1, everyone if level + 1 < last else seconds)
+
     @when_second
     def _():
-        for index in range(3):
+        pair_copy(2).wait_recv()
+        wait_out(SRC)
+        for at in everyone:
+            waves[0, SRC, REACH + at, inside, :] = arrived_rows(SRC, 0, at)
+        begin(SRC)
+
+    advance_rcv(1)
+
+    @when_second
+    def _():
+        for index in range(2):
             pair_copy(index).wait_recv()
         for side in (LEFT, RIGHT):
             wait_halo(ALT, 0, side)
-        arrived = landed.at[pl.ds(0, (devices - 1) * block)]
-        pltpu.make_async_copy(arrived, arrived, out_recv).wait()
+        wait_out(ALT)
         for at in everyone:
-            waves[0, SRC, REACH + at, inside, :] = arrived_rows(0, at)
-        for field in FIELDS:
-            if field == ALT:
-                for at in everyone:
-                    for part in range(PARTS):
-                        medium_alt[part, at] = arrived_rows(PARTS + part, at)
-            local(field, 0, everyone)
-            finish(field, 0, everyone)
-            for side in (RIGHT, LEFT):
-                send_halo(field, 1, side)
+            for part in range(PARTS):
+                medium_alt[part, at] = arrived_rows(ALT, part, at)
+        begin(ALT)
         pair_copy(3).start()
-        local_both(1, everyone)
-        for field in FIELDS:
-            for side in (LEFT, RIGHT):
-                wait_sent(field, 1, side)
-
-    advance_rcv(1)
+
     for level in range(1, last):
 
         @when_second
         def _():
-            for field in FIELDS:
-                for side in (LEFT, RIGHT):
-                    wait_halo(field, level, side)
-                finish(field, level, everyone)
-                for side in (RIGHT, LEFT):
-                    send_halo(field, level + 1, side)
+            go_on(SRC, level)
+
+        @when_second
+        def _():
+            go_on(ALT, level)
             if level + 1 == last - 1:
                 pair_copy(4).start()
             if level + 1 == last:
                 pair_copy(5).start()
-            local_both(level + 1, everyone if level + 1 < last else seconds)
-            for field in FIELDS:
-                for side in (LEFT, RIGHT):
-                    wait_sent(field, level + 1, side)
 
         advance_rcv(level + 1)
-
     @when_first
     def _():
         for index in (3, 4):
@@ -521,17 +538,23 @@
 
     @when_first
     def _():
-        sent = staged.at[pl.ds(0, pairs * block)]
-        pltpu.make_async_copy(sent, sent, out_send).wait()
+        for field in FIELDS:
+            sent = staged.at[field, pl.ds(0, pairs * block)]
+            pltpu.make_async_copy(sent, sent, out_send.at[field]).wait()
         wait_sent(ALT, 0, RIGHT)
         for index in range(3):
             pair_copy(index).wait_send()
 
     @when_second
     def _():
-        sent = staged.at[pl.ds(0, (pairs - 1) * block)]
-        pltpu.make_async_copy(sent, sent, out_send).wait()
+        for field in FIELDS:
+            sent = staged.at[field, pl.ds(0, (pairs - 1) * block)]
+            pltpu.make_async_copy(sent, sent, out_send.at[field]).wait()
         wait_sent(ALT, 0, LEFT)
+        for level in range(1, steps):
+            for field in FIELDS:
+                for side in (LEFT, RIGHT):
+                    wait_sent(field, level, side)
         for index in range(3, 6):
             pair_copy(index).wait_send()
 
@@ -562,7 +585,7 @@
         steps = wavelet.shape[0]
         lags = lag_order.shape[0]
         half = (lags - 1) // 2
-        rows = 4 * PARTS * slab
+        rows = 2 * PARTS * slab
         f32 = jnp.float32
         vmem = pl.BlockSpec(memory_space=pltpu.VMEM)
         hbm = pl.BlockSpec(memory_space=pltpu.HBM)
@@ -588,8 +611,8 @@
             like(rec_x),
             scalars(lag_order),
             pltpu.VMEM((taken, 2, slab, cells + 2 * half, cells_z), f32),
-            pltpu.VMEM((devices // 2 * slab * rows, cells_z), f32),
-            pltpu.VMEM((devices * slab * rows, cells_z), f32),
+            pltpu.VMEM((2, devices // 2 * slab * rows, cells_z), f32),
+            pltpu.VMEM((2, devices * slab * rows, cells_z), f32),
             wide(steps + 1, 2, both + 2 * REACH),
             wide(steps + 1, slab + 2 * REACH),
             field(PARTS, both),
@@ -604,7 +627,7 @@
             in_specs=[hbm] * 10,
             out_specs=(vmem,) * 5,
             scratch_shapes=scratch
-            + [pltpu.SemaphoreType.DMA] * 2
+            + [pltpu.SemaphoreType.DMA((2,))] * 2
             + [pltpu.SemaphoreType.DMA((2, steps, 2))] * 2
             + [pltpu.SemaphoreType.DMA((steps, 2))] * 2
             + [pltpu.SemaphoreType.DMA((6,))] * 2

time: 21.7 us -> 20.7 us (0.954)
  Pallas kernels: 20.9 us -> 19.8 us
    pallas_call x1, Pallas kernels: 19.9 us -> 18.7 us  [on_device(): pl.pallas_call(functools.partial(window_kernel, devices), out_shape=shape...]
where the time goes in v3:
time: 20.7 us; the launch traced here: 20.4 us
  Pallas kernels  19.8 us (96%)
  between operations  0.64 us (3%)
    pallas_call x1, Pallas kernels, on_device(): pl.pallas_call(functools.partial(window_kernel, devices), out_shape=shape...  18.7 us
    pallas_call x1, Pallas kernels, on_device(): pl.pallas_call(deliver_kernel, out_shape=shapes, in_specs=[vmem] * 5, out...  1.07 us

profile of v3, /device:TPU:1, one launch (start us, length us, event | category | flops | bytes accessed | tf_op | source)
XLA Modules:
  0.0 20.4 jit_solution(18342738660439658122)
XLA Ops:
  0.6 18.7 %window.1 = (f32[2,32,128]{2,1,0:T(8,128)S(1)}, f32[2,32,128]{2,1,0:T(8,128)S(1)}, f32[2,32,128]{2,1,0:T(8,128)S(1)}, f32[2,32,128]{2,1,0:T(8,128)S(1)}, f32[33,2,32,128]{3,2,1,0:T(8,128)S(1)}) custom-call(f32[2,32,128]{2,1,0:T(8,128)} %src_now_in.1, f32[2,32,128]{2,1,0:T(8,128)} %src_old_in.1, f32[2,32,128]{2,1,0:T(8,128)} %bitcast.8, ...), custom_call_target="tpu_custom_call" | custom-call | tf_op jit(solution)/shard_map/window/pallas_call | solution.py:624
  19.4 1.1 %deliver.1 = (f32[2,32,128]{2,1,0:T(8,128)}, f32[2,32,128]{2,1,0:T(8,128)}, f32[2,32,128]{2,1,0:T(8,128)}, f32[2,32,128]{2,1,0:T(8,128)}, f32[33,2,32,128]{3,2,1,0:T(8,128)}) custom-call(f32[2,32,128]{2,1,0:T(8,128)S(1)} %get-tuple-element.15.refs_0_, f32[2,32,128]{2,1,0:T(8,128)S(1)} %get-tuple-element.16.refs_1_, ...), custom_call_target="tpu_custom_call" | custom-call | tf_op jit(solution)/shard_map/deliver/pallas_call | solution.py:656

commit v4 on v3

--- a/solution.py
+++ b/solution.py
@@ -157,7 +157,7 @@
 
         return second(window)
 
-    for load in loads[:3]:
+    for load in loads[:2]:
         load.wait()
     for at in range(slab):
         def now_rows(where):
@@ -174,12 +174,6 @@
                 into = at * rows + part * both + y
                 staged[SRC, pl.ds(into, pairs, stride=block), :] = partial[
                     part, at, pl.ds(y, pairs, stride=both), :
-                ]
-        for part in range(PARTS):
-            for x in range(both):
-                into = at * rows + part * both + x
-                staged[ALT, pl.ds(into, pairs, stride=block), :] = medium[
-                    part, odd * slab + at, pl.ds(x, pairs, stride=both), :
                 ]
 
     pl.semaphore_wait(barrier, pairs + odd * (pair < pairs - 1).astype(jnp.int32))
@@ -268,9 +262,20 @@
     loads[3].wait()
     send_echo(0)
 
-    for field in FIELDS:
-        for distance in far_pairs:
+    def send_out(field):
+        for distance in far_pairs[::-1]:
             out_copy(field, lax.rem(pair + distance, pairs)).start()
+
+    send_out(SRC)
+    loads[2].wait()
+    for at in range(slab):
+        for part in range(PARTS):
+            for x in range(both):
+                into = at * rows + part * both + x
+                staged[ALT, pl.ds(into, pairs, stride=block), :] = medium[
+                    part, odd * slab + at, pl.ds(x, pairs, stride=both), :
+                ]
+    send_out(ALT)
 
     for load in loads[4:]:
         load.wait()
@@ -445,9 +450,9 @@
         pltpu.make_async_copy(arrived, arrived, out_recv.at[field]).wait()
 
     def begin(field):
-        local(field, 0, everyone)
-        finish(field, 0, everyone)
-        for side in (RIGHT, LEFT):
+        for side, ats in ((RIGHT, firsts), (LEFT, seconds)):
+            local(field, 0, ats)
+            finish(field, 0, ats)
             send_halo(field, 1, side)
         local(field, 1, everyone)
 
@@ -497,6 +502,8 @@
                 pair_copy(4).start()
             if level + 1 == last:
                 pair_copy(5).start()
+            for side in (LEFT, RIGHT):
+                wait_sent(ALT, level + 1, side)
 
         advance_rcv(level + 1)
     @when_first
@@ -551,10 +558,10 @@
             sent = staged.at[field, pl.ds(0, (pairs - 1) * block)]
             pltpu.make_async_copy(sent, sent, out_send.at[field]).wait()
         wait_sent(ALT, 0, LEFT)
-        for level in range(1, steps):
-            for field in FIELDS:
-                for side in (LEFT, RIGHT):
-                    wait_sent(field, level, side)
+        for side in (LEFT, RIGHT):
+            wait_sent(ALT, 1, side)
+            for level in range(1, steps):
+                wait_sent(SRC, level, side)
         for index in range(3, 6):
             pair_copy(index).wait_send()
 

time: 20.7 us -> 20.5 us (level)
  no operation moved by 1% of the time
where the time goes in v4:
time: 20.5 us; the launch traced here: 20.2 us
  Pallas kernels  19.6 us (96%)
  between operations  0.64 us (3%)
    pallas_call x1, Pallas kernels, on_device(): pl.pallas_call(functools.partial(window_kernel, devices), out_shape=shape...  18.5 us
    pallas_call x1, Pallas kernels, on_device(): pl.pallas_call(deliver_kernel, out_shape=shapes, in_specs=[vmem] * 5, out...  1.07 us

profile of v4, /device:TPU:1, one launch (start us, length us, event | category | flops | bytes accessed | tf_op | source)
XLA Modules:
  0.0 20.2 jit_solution(12145286490547272786)
XLA Ops:
  0.6 18.5 %window.1 = (f32[2,32,128]{2,1,0:T(8,128)S(1)}, f32[2,32,128]{2,1,0:T(8,128)S(1)}, f32[2,32,128]{2,1,0:T(8,128)S(1)}, f32[2,32,128]{2,1,0:T(8,128)S(1)}, f32[33,2,32,128]{3,2,1,0:T(8,128)S(1)}) custom-call(f32[2,32,128]{2,1,0:T(8,128)} %src_now_in.1, f32[2,32,128]{2,1,0:T(8,128)} %src_old_in.1, f32[2,32,128]{2,1,0:T(8,128)} %bitcast.8, ...), custom_call_target="tpu_custom_call" | custom-call | tf_op jit(solution)/shard_map/window/pallas_call | solution.py:631
  19.2 1.1 %deliver.1 = (f32[2,32,128]{2,1,0:T(8,128)}, f32[2,32,128]{2,1,0:T(8,128)}, f32[2,32,128]{2,1,0:T(8,128)}, f32[2,32,128]{2,1,0:T(8,128)}, f32[33,2,32,128]{3,2,1,0:T(8,128)}) custom-call(f32[2,32,128]{2,1,0:T(8,128)S(1)} %get-tuple-element.15.refs_0_, f32[2,32,128]{2,1,0:T(8,128)S(1)} %get-tuple-element.16.refs_1_, ...), custom_call_target="tpu_custom_call" | custom-call | tf_op jit(solution)/shard_map/deliver/pallas_call | solution.py:663

commit v5 on v4

--- a/solution.py
+++ b/solution.py
@@ -138,15 +138,9 @@
     zero_plane = jnp.zeros((cells, cells_z), jnp.float32)
     zero_half = jnp.zeros((half, cells_z), jnp.float32)
 
-    for field in FIELDS:
-        for level in range(steps):
-            for at in range(REACH, REACH + both):
-                waves[level, field, at, 0:EDGE, :] = zero_edge
-                waves[level, field, at, EDGE + cells : EDGE + cells + EDGE, :] = zero_edge
-    for level in range(steps):
-        for at in range(REACH, REACH + slab):
-            echoes[level, at, 0:EDGE, :] = zero_edge
-            echoes[level, at, EDGE + cells : EDGE + cells + EDGE, :] = zero_edge
+    for at in range(REACH, REACH + both):
+        waves[0, ALT, at, 0:EDGE, :] = zero_edge
+        waves[0, ALT, at, EDGE + cells : EDGE + cells + EDGE, :] = zero_edge
 
     row_at = lax.broadcasted_iota(jnp.int32, (cells, cells_z), 0)
     lane_at = lax.broadcasted_iota(jnp.int32, (cells, cells_z), 1)
@@ -277,6 +271,16 @@
                 ]
     send_out(ALT)
 
+    for field in FIELDS:
+        for level in range(steps):
+            for at in range(REACH, REACH + both):
+                waves[level, field, at, 0:EDGE, :] = zero_edge
+                waves[level, field, at, EDGE + cells : EDGE + cells + EDGE, :] = zero_edge
+    for level in range(steps):
+        for at in range(REACH, REACH + slab):
+            echoes[level, at, 0:EDGE, :] = zero_edge
+            echoes[level, at, EDGE + cells : EDGE + cells + EDGE, :] = zero_edge
+
     for load in loads[4:]:
         load.wait()
 
@@ -502,8 +506,6 @@
                 pair_copy(4).start()
             if level + 1 == last:
                 pair_copy(5).start()
-            for side in (LEFT, RIGHT):
-                wait_sent(ALT, level + 1, side)
 
         advance_rcv(level + 1)
     @when_first
@@ -558,10 +560,10 @@
             sent = staged.at[field, pl.ds(0, (pairs - 1) * block)]
             pltpu.make_async_copy(sent, sent, out_send.at[field]).wait()
         wait_sent(ALT, 0, LEFT)
-        for side in (LEFT, RIGHT):
-            wait_sent(ALT, 1, side)
-            for level in range(1, steps):
-                wait_sent(SRC, level, side)
+        for level in range(1, steps):
+            for field in FIELDS:
+                for side in (LEFT, RIGHT):
+                    wait_sent(field, level, side)
         for index in range(3, 6):
             pair_copy(index).wait_send()
 

time: 20.5 us -> 20.4 us (level)
  no operation moved by 1% of the time
where the time goes in v5:
time: 20.4 us; the launch traced here: 20.3 us
  Pallas kernels  19.6 us (96%)
  between operations  0.64 us (3%)
    pallas_call x1, Pallas kernels, on_device(): pl.pallas_call(functools.partial(window_kernel, devices), out_shape=shape...  18.5 us
    pallas_call x1, Pallas kernels, on_device(): pl.pallas_call(deliver_kernel, out_shape=shapes, in_specs=[vmem] * 5, out...  1.07 us

profile of v5, /device:TPU:1, one launch (start us, length us, event | category | flops | bytes accessed | tf_op | source)
XLA Modules:
  0.0 20.3 jit_solution(7160896911789260170)
XLA Ops:
  0.6 18.5 %window.1 = (f32[2,32,128]{2,1,0:T(8,128)S(1)}, f32[2,32,128]{2,1,0:T(8,128)S(1)}, f32[2,32,128]{2,1,0:T(8,128)S(1)}, f32[2,32,128]{2,1,0:T(8,128)S(1)}, f32[33,2,32,128]{3,2,1,0:T(8,128)S(1)}) custom-call(f32[2,32,128]{2,1,0:T(8,128)} %src_now_in.1, f32[2,32,128]{2,1,0:T(8,128)} %src_old_in.1, f32[2,32,128]{2,1,0:T(8,128)} %bitcast.8, ...), custom_call_target="tpu_custom_call" | custom-call | tf_op jit(solution)/shard_map/window/pallas_call | solution.py:633
  19.2 1.1 %deliver.1 = (f32[2,32,128]{2,1,0:T(8,128)}, f32[2,32,128]{2,1,0:T(8,128)}, f32[2,32,128]{2,1,0:T(8,128)}, f32[2,32,128]{2,1,0:T(8,128)}, f32[33,2,32,128]{3,2,1,0:T(8,128)}) custom-call(f32[2,32,128]{2,1,0:T(8,128)S(1)} %get-tuple-element.15.refs_0_, f32[2,32,128]{2,1,0:T(8,128)S(1)} %get-tuple-element.16.refs_1_, ...), custom_call_target="tpu_custom_call" | custom-call | tf_op jit(solution)/shard_map/deliver/pallas_call | solution.py:665

commit v6 on v5

--- a/solution.py
+++ b/solution.py
@@ -302,12 +302,6 @@
             ]
 
 
-    for snap in range(padded.shape[0]):
-        for field in range(2):
-            for y in range(slab):
-                padded[snap, field, y, 0:half, :] = zero_half
-                padded[snap, field, y, half + cells : 2 * half + cells, :] = zero_half
-
     def clear_planes(first):
         for level in range(steps):
             for field in FIELDS:
@@ -448,6 +442,11 @@
 
     local_rcv(0)
     advance_rcv(0)
+    for snap in range(padded.shape[0]):
+        for field in range(2):
+            for y in range(slab):
+                padded[snap, field, y, 0:half, :] = zero_half
+                padded[snap, field, y, half + cells : 2 * half + cells, :] = zero_half
 
     def wait_out(field):
         arrived = landed.at[field, pl.ds(0, (devices - 1) * block)]

time: 20.4 us -> 20.4 us (level)
  no operation moved by 1% of the time
where the time goes in v6:
time: 20.4 us; the launch traced here: 20.3 us
  Pallas kernels  19.6 us (96%)
  between operations  0.64 us (3%)
    pallas_call x1, Pallas kernels, on_device(): pl.pallas_call(functools.partial(window_kernel, devices), out_shape=shape...  18.5 us
    pallas_call x1, Pallas kernels, on_device(): pl.pallas_call(deliver_kernel, out_shape=shapes, in_specs=[vmem] * 5, out...  1.07 us

profile of v6, /device:TPU:1, one launch (start us, length us, event | category | flops | bytes accessed | tf_op | source)
XLA Modules:
  0.0 20.3 jit_solution(16992181136116765857)
XLA Ops:
  0.6 18.5 %window.1 = (f32[2,32,128]{2,1,0:T(8,128)S(1)}, f32[2,32,128]{2,1,0:T(8,128)S(1)}, f32[2,32,128]{2,1,0:T(8,128)S(1)}, f32[2,32,128]{2,1,0:T(8,128)S(1)}, f32[33,2,32,128]{3,2,1,0:T(8,128)S(1)}) custom-call(f32[2,32,128]{2,1,0:T(8,128)} %src_now_in.1, f32[2,32,128]{2,1,0:T(8,128)} %src_old_in.1, f32[2,32,128]{2,1,0:T(8,128)} %bitcast.8, ...), custom_call_target="tpu_custom_call" | custom-call | tf_op jit(solution)/shard_map/window/pallas_call | solution.py:632
  19.2 1.1 %deliver.1 = (f32[2,32,128]{2,1,0:T(8,128)}, f32[2,32,128]{2,1,0:T(8,128)}, f32[2,32,128]{2,1,0:T(8,128)}, f32[2,32,128]{2,1,0:T(8,128)}, f32[33,2,32,128]{3,2,1,0:T(8,128)}) custom-call(f32[2,32,128]{2,1,0:T(8,128)S(1)} %get-tuple-element.15.refs_0_, f32[2,32,128]{2,1,0:T(8,128)S(1)} %get-tuple-element.16.refs_1_, ...), custom_call_target="tpu_custom_call" | custom-call | tf_op jit(solution)/shard_map/deliver/pallas_call | solution.py:664
